TPU v7x, 256 devices: a whole 4x4x8 slice. The times are simulated.
256 devices in a mesh: req: 4 (over x), exp: 64 (over z, y, core).
Axes of the slice: x: 4, y: 4, z: 8, core: 2. Of those that a mesh axis runs over, the one named last changes fastest.
Arguments:
- hidden: bfloat16 [256, 32, 2048], P(('req', 'exp')), may hold values from -6 to 6
- queries: bfloat16 [256, 32, 3072], P(('req', 'exp'))
- new_latent: bfloat16 [256, 32, 576], P(('req', 'exp')), may hold values from -6 to 6
- pages: bfloat16 [2048, 128, 576], P(('req', 'exp'))
- page_table: int32 [256, 8], P(('req', 'exp')), may hold values from 0 to 7, each once within a row
- cache_len: int32 [256], P(('req', 'exp')), may hold values from 1 to 992, as said below
- parents: int32 [256, 32], P(('req', 'exp')), may hold values from 0 to 30, as said below
- accept_path: int32 [256, 32], P(('req', 'exp')), may hold values from 0 to 31, as said below
- accept_count: int32 [256], P(('req', 'exp')), may hold values from 1 to 32, as said below
- key_up: bfloat16 [16, 128, 512], replicated, may hold values from -0.5 to 0.5
- value_up: bfloat16 [16, 512, 128], replicated, may hold values from -0.25 to 0.25
- out_proj: bfloat16 [2048, 2048], P(None, 'req'), may hold values from -0.125 to 0.125
- norm_gain: bfloat16 [2048], replicated, may hold values from 0.5 to 1.5
- route_ids: int32 [4, 64, 32, 6], P(None, 'exp'), may hold values from 0 to 63, all different within a row; in each aligned block of 32 rows (0 to 31, 32 to 63, ..., all dimensions but the last counted through in order) at most 6 rows name the same one
- route_weights: float32 [4, 64, 32, 6], P(None, 'exp'), may hold values from 0.2 to 1.2
- w_gate: bfloat16 [64, 2048, 1408], P('exp', None, 'req'), may hold values from -0.125 to 0.125
- w_up: bfloat16 [64, 2048, 1408], P('exp', None, 'req'), may hold values from -0.125 to 0.125
- w_down: bfloat16 [64, 1408, 2048], P('exp', 'req'), may hold values from -0.15625 to 0.15625
Outputs:
- layer_out: bfloat16 [256, 32, 2048], P(('req', 'exp'))
- new_pages: bfloat16 [2048, 128, 576], P(('req', 'exp'))
Inputs may be any that keep to these rules, and one draw needn't show every extreme that they name: `route_ids`: in each request no expert is named by more than 6 tokens, a bound that some block reaches. `page_table`: each row is an order of the 8 pages of the request's pool. `cache_len`: some request holds the largest length. parents[q, 0] = 0; for t >= 1 the parent of t is below t; one request's tree is a single chain. `accept_path`: entry k for k < accept_count is the ancestor at depth k of the last accepted token, entry 0 the root; later entries are 0. `accept_count`: one more than the depth of the last accepted token.
All inputs are finite; a program needn't handle non-finite values.
Results may differ from a plain program's by a relative error of at most 0.023.
Values may be sent and summed in bfloat16 or wider, within the bound.
A program may use at most 128 MiB of HBM per device.

v0:
```python
import math
import jax
import jax.numpy as jnp
from jax import lax
from jax.sharding import PartitionSpec as P

TOP = 6
TREE = 32


def ancestry(parent_row):
    count = parent_row.shape[0]
    ident = jnp.eye(count, dtype=jnp.int32)
    linked = (parent_row[:, None] == jnp.arange(count, dtype=jnp.int32)[None, :]).astype(jnp.int32)
    reach = jnp.minimum(ident + linked, 1)
    for sweep in range(count.bit_length()):
        reach = jnp.minimum(jnp.dot(reach, reach), 1)
    return reach


def attend(query_row, page_pool, table_row, length, parent_row, fresh, key_up, value_up):
    count = query_row.shape[0]
    heads = key_up.shape[0]
    nope = key_up.shape[1]
    latent = key_up.shape[2]
    shaped = query_row.reshape(count, heads, -1)
    scale = 1.0 / math.sqrt(shaped.shape[2])
    q_nope = shaped[:, :, :nope]
    q_rope = shaped[:, :, nope:]
    q_latent = jnp.einsum(
        "thn,hnc->thc", q_nope, key_up, preferred_element_type=jnp.float32
    ).astype(jnp.bfloat16)
    q_full = jnp.concatenate([q_latent, q_rope], axis=2)
    cache_rows = jnp.take(page_pool, table_row, axis=0).reshape(-1, page_pool.shape[2])
    score_cache = (
        jnp.einsum("thc,kc->thk", q_full, cache_rows, preferred_element_type=jnp.float32) * scale
    )
    score_tree = (
        jnp.einsum("thc,jc->thj", q_full, fresh, preferred_element_type=jnp.float32) * scale
    )
    live = jnp.arange(cache_rows.shape[0], dtype=jnp.int32) < length
    score_cache = jnp.where(live[None, None, :], score_cache, -1e30)
    score_tree = jnp.where(ancestry(parent_row)[:, None, :] > 0, score_tree, -1e30)
    peak = jnp.maximum(jnp.max(score_cache, axis=2), jnp.max(score_tree, axis=2))[:, :, None]
    exp_cache = jnp.exp(score_cache - peak)
    exp_tree = jnp.exp(score_tree - peak)
    total = jnp.sum(exp_cache, axis=2, keepdims=True) + jnp.sum(exp_tree, axis=2, keepdims=True)
    prob_cache = (exp_cache / total).astype(jnp.bfloat16)
    prob_tree = (exp_tree / total).astype(jnp.bfloat16)
    context = jnp.einsum(
        "thk,kc->thc", prob_cache, cache_rows[:, :latent], preferred_element_type=jnp.float32
    )
    context = context + jnp.einsum(
        "thj,jc->thc", prob_tree, fresh[:, :latent], preferred_element_type=jnp.float32
    )
    context = context.astype(jnp.bfloat16)
    head_out = jnp.einsum(
        "thc,hcv->thv", context, value_up, preferred_element_type=jnp.float32
    ).astype(jnp.bfloat16)
    return head_out.reshape(count, -1)


def write_rows(page_pool, table_row, length, path_row, count, fresh):
    pool_len = page_pool.shape[0]
    page_size = page_pool.shape[1]
    pool_ids = jnp.arange(pool_len, dtype=jnp.int32)
    match = table_row[None, :] == pool_ids[:, None]
    logical = jnp.sum(jnp.where(match, pool_ids[None, :], 0), axis=1)
    position = logical[:, None] * page_size + jnp.arange(page_size, dtype=jnp.int32)[None, :]
    offset = position - length
    valid = (offset >= 0) & (offset < count)
    source = jnp.take(path_row, jnp.clip(offset, 0, path_row.shape[0] - 1))
    written = jnp.take(fresh, source, axis=0)
    return jnp.where(valid[:, :, None], written, page_pool)


def slot_tables(route_rows, weight_rows, experts, capacity):
    expert_ids = jnp.arange(experts, dtype=jnp.int32)
    hits = route_rows[:, :, :, None] == expert_ids
    chosen = jnp.sum(hits.astype(jnp.int32), axis=2)
    weight_by = jnp.sum(jnp.where(hits, weight_rows[:, :, :, None], 0.0), axis=2)
    before = jnp.cumsum(chosen, axis=1) - chosen
    chosen_t = jnp.transpose(chosen, (0, 2, 1))
    before_t = jnp.transpose(before, (0, 2, 1))
    weight_t = jnp.transpose(weight_by, (0, 2, 1))
    slot_ids = jnp.arange(capacity, dtype=jnp.int32)
    placed = (chosen_t[:, :, None, :] > 0) & (
        before_t[:, :, None, :] == slot_ids[None, None, :, None]
    )
    weighted = jnp.where(placed, weight_t[:, :, None, :], 0.0)
    return (placed.astype(jnp.bfloat16), weighted)


def local(
    hidden,
    queries,
    new_latent,
    pages,
    page_table,
    cache_len,
    parents,
    accept_path,
    accept_count,
    key_up,
    value_up,
    out_proj,
    norm_gain,
    route_ids,
    route_weights,
    w_gate,
    w_up,
    w_down,
):
    width = hidden.shape[2]
    head_out = attend(
        queries[0], pages, page_table[0], cache_len[0], parents[0], new_latent[0], key_up, value_up
    )
    column_block = jnp.dot(
        lax.all_gather(head_out, "req", axis=0, tiled=True),
        out_proj,
        preferred_element_type=jnp.float32,
    ).astype(jnp.bfloat16)
    projected = lax.all_to_all(column_block, "req", split_axis=0, concat_axis=1, tiled=True)
    mixed = (hidden[0].astype(jnp.float32) + projected.astype(jnp.float32)).astype(jnp.bfloat16)
    mixed_f = mixed.astype(jnp.float32)
    normed = (
        mixed_f
        * lax.rsqrt(jnp.mean(mixed_f * mixed_f, axis=1, keepdims=True) + 1e-06)
        * norm_gain.astype(jnp.float32)
    ).astype(jnp.bfloat16)
    experts = lax.axis_size("exp") * w_gate.shape[0]
    capacity = max(2, min(TREE, 2 * TREE * TOP // experts))
    gate_local = w_gate[0]
    up_local = w_up[0]
    down_local = w_down[0]
    copies = lax.all_gather(normed[None], "req", axis=0, tiled=True)
    placed, weighted = slot_tables(route_ids[:, 0], route_weights[:, 0], experts, capacity)
    outbound = jnp.einsum(
        "gxct,gtd->xgcd", placed, copies, preferred_element_type=jnp.float32
    ).astype(jnp.bfloat16)
    slot_block = lax.all_to_all(outbound, "exp", split_axis=0, concat_axis=0, tiled=True)
    flat = slot_block.reshape(-1, width)
    gate_val = jnp.dot(flat, gate_local, preferred_element_type=jnp.float32)
    up_val = jnp.dot(flat, up_local, preferred_element_type=jnp.float32)
    active = (jax.nn.silu(gate_val) * up_val).astype(jnp.bfloat16)
    returned = lax.all_to_all(
        jnp.dot(active, down_local, preferred_element_type=jnp.float32)
        .astype(jnp.bfloat16)
        .reshape(slot_block.shape),
        "exp",
        split_axis=0,
        concat_axis=0,
        tiled=True,
    )
    partial_value = jnp.einsum("gxct,xgcd->gtd", weighted, returned.astype(jnp.float32))
    moe = lax.psum_scatter(
        partial_value.astype(jnp.bfloat16), "req", scatter_dimension=0, tiled=True
    ).astype(jnp.float32)[0]
    layer_out = (mixed_f + moe).astype(jnp.bfloat16)[None]
    new_pool = write_rows(
        pages, page_table[0], cache_len[0], accept_path[0], accept_count[0], new_latent[0]
    )
    return (layer_out, new_pool)


def solution(mesh):
    in_specs = (
        P(("req", "exp"), None, None),
        P(("req", "exp"), None, None),
        P(("req", "exp"), None, None),
        P(("req", "exp"), None, None),
        P(("req", "exp"), None),
        P(("req", "exp")),
        P(("req", "exp"), None),
        P(("req", "exp"), None),
        P(("req", "exp")),
        P(),
        P(),
        P(None, "req"),
        P(),
        P(None, "exp", None, None),
        P(None, "exp", None, None),
        P("exp", None, "req"),
        P("exp", None, "req"),
        P("exp", "req", None),
    )
    out_specs = (P(("req", "exp"), None, None), P(("req", "exp"), None, None))
    return jax.shard_map(local, mesh=mesh, in_specs=in_specs, out_specs=out_specs, check_vma=False)
```

profile of v0, /device:TPU:8, one launch (start us, length us, event | category | flops | bytes accessed | tf_op | source)
XLA Modules:
  0.0 495.9 jit_solution(1943214140383278034)
XLA Ops:
  7.2 1.4 reshape_squeeze.3
  11.4 1.7 gather_fusion
  13.1 2.4 copy.166
  16.0 0.8 copy-done.6
  17.3 2.4 fusion.9
  21.8 2.1 fusion.10
  24.2 2.1 divide_convert_fusion
  26.3 1.8 fusion.24
  28.1 2.5 fusion.22
  30.6 13.1 %all_gather.6 = bf16[128,2048]{1,0:T(8,128)(2,1)S(1)} all-gather(bf16[32,2048]{1,0:T(8,128)(2,1)S(1)} %bitcast.125), channel_id=1, replica_groups=mesh['req'=4,'exp'=64] {'req'}, dimensions={0}, use_global_device_ids=true | all-gather | bytes 655360 | tf_op jit(solution)/shard_map/all_gather | solution.py:119
  43.8 2.7 convolution_convert_fusion.2
  46.5 4.4 all-to-all-start
  51.2 5.6 %all-to-all-done = bf16[4,32,512]{2,1,0:T(8,128)(2,1)S(1)} async-done(((bf16[4,32,512]{2,1,0:T(8,128)(2,1)}), bf16[4,32,512]{2,1,0:T(8,128)(2,1)S(1)}, u32[]{:S(2)}, u32[]{:S(2)}) %all-to-all-start) | async-done | bytes 131104 | tf_op jit(solution)/shard_map/all_to_all | solution.py:123
  57.6 13.7 %all_gather.7 = bf16[4,32,2048]{2,1,0:T(8,128)(2,1)S(1)} all-gather(bf16[1,32,2048]{2,1,0:T(8,128)(2,1)S(1)} %fusion.38), channel_id=1, replica_groups=mesh['req'=4,'exp'=64] {'req'}, dimensions={0}, use_global_device_ids=true | all-gather | bytes 655360 | tf_op jit(solution)/shard_map/all_gather | solution.py:136
  71.3 4.5 convert_bitcast_fusion
  75.8 10.3 %copy.157 = bf16[64,4,6,2048]{3,1,2,0:T(4,128)(2,1)} copy(bf16[64,4,6,2048]{3,0,2,1:T(8,128)(2,1)} %convert_bitcast_fusion) | data formatting | bytes 12582912 | tf_op jit(solution)/shard_map/convert_element_type | solution.py:140
  86.1 153.4 %all_to_all.23 = bf16[64,4,6,2048]{3,1,2,0:T(4,128)(2,1)S(1)} all-to-all(bf16[64,4,6,2048]{3,1,2,0:T(4,128)(2,1)} %copy.157), channel_id=1, replica_groups=mesh['req'=4,'exp'=64] {'exp'}, dimensions={0} | all-to-all | bytes 12582912 | tf_op jit(solution)/shard_map/all_to_all | solution.py:141
  239.5 10.7 %copy.158 = bf16[64,4,6,2048]{3,2,1,0:T(8,128)(2,1)} copy(bf16[64,4,6,2048]{3,1,2,0:T(4,128)(2,1)S(1)} %all_to_all.23) | data formatting | bytes 12582912 | tf_op jit(solution)/shard_map/all_to_all | solution.py:141
  250.2 11.1 %reshape.257 = bf16[1536,2048]{1,0:T(8,128)(2,1)} reshape(bf16[64,4,6,2048]{3,2,1,0:T(8,128)(2,1)} %copy.158) | data formatting | bytes 12582912 | tf_op jit(solution)/shard_map/reshape | solution.py:142
  261.3 7.0 %fusion.13 = f32[1536,352]{0,1:T(8,128)} fusion(bf16[1536,2048]{1,0:T(8,128)(2,1)} %reshape.257, bf16[1,2048,352]{1,2,0:T(8,128)(2,1)} %param.33), kind=kOutput, calls=%fused_computation.18 | convolution fusion | flops 2214592512 | bytes 9895936 | tf_op jit(solution)/shard_map/dot_general | solution.py:143
  268.3 12.2 %convolution_convert_fusion = bf16[1536,2048]{1,0:T(8,128)(2,1)} fusion(bf16[1,352,2048]{2,1,0:T(8,128)(2,1)} %param.35, bf16[1536,2048]{1,0:T(8,128)(2,1)} %reshape.257, f32[1536,352]{0,1:T(8,128)} %fusion.13, bf16[1,2048,352]{1,2,0:T(8,128)(2,1)} %param.34), kind=kOutput, calls=%fused_computation.3 | convolution fusion | flops 4435574784 | bytes 17629184 | tf_op jit(solution)/shard_map/dot_general | solution.py:147
  280.4 11.4 %reshape.258 = bf16[64,4,6,2048]{3,2,1,0:T(8,128)(2,1)} reshape(bf16[1536,2048]{1,0:T(8,128)(2,1)} %convolution_convert_fusion) | data formatting | bytes 12582912 | tf_op jit(solution)/shard_map/reshape | solution.py:149
  291.8 18.8 %copy.159 = bf16[64,4,6,2048]{3,1,2,0:T(4,128)(2,1)} copy(bf16[64,4,6,2048]{3,2,1,0:T(8,128)(2,1)} %reshape.258) | data formatting | bytes 12582912 | tf_op jit(solution)/shard_map/reshape | solution.py:149
  310.7 5.7 %all-to-all-start.2 = ((bf16[64,4,6,2048]{3,1,2,0:T(4,128)(2,1)}), bf16[64,4,6,2048]{3,1,2,0:T(4,128)(2,1)}, u32[]{:S(2)}, u32[]{:S(2)}) async-start(bf16[64,4,6,2048]{3,1,2,0:T(4,128)(2,1)} %copy.159), calls=%async_computation.2 | async-start | bytes 12582912 | tf_op jit(solution)/shard_map/all_to_all | solution.py:146
  316.9 140.8 %all-to-all-done.2 = bf16[64,4,6,2048]{3,1,2,0:T(4,128)(2,1)} async-done(((bf16[64,4,6,2048]{3,1,2,0:T(4,128)(2,1)}), bf16[64,4,6,2048]{3,1,2,0:T(4,128)(2,1)}, u32[]{:S(2)}, u32[]{:S(2)}) %all-to-all-start.2) | async-done | bytes 6291488 | tf_op jit(solution)/shard_map/all_to_all | solution.py:146
  457.7 10.5 %fusion.6 = bf16[4,32,2048]{2,1,0:T(8,128)(2,1)} fusion(bf16[64,4,6,2048]{3,1,2,0:T(4,128)(2,1)} %all-to-all-done.2, bf16[4,64,32]{1,2,0:T(8,128)(2,1)S(1)} %bitcast.128, s32[4,64,32]{1,2,0:T(8,128)S(1)} %subtract_bitcast_fusion, pred[4,64,32]{1,2,0:T(8,128)(4,1)S(1)} %compare_bitcast_fusion), kind=kOutput, calls=%fused_computation.10 | convolution fusion | flops 201474048 | bytes 6873088 | tf_op jit(solution)/shard_map/gxct,xgcd->gtd/dot_general | solution.py:155
  468.8 6.6 %gather_fusion.1 = s32[1024]{0:T(1024)S(1)} fusion(s32[32]{0:T(128)S(1)} %bitcast.120, s32[1024]{0:T(1024)S(1)} %bitcast_clamp_fusion), kind=kCustom, calls=%fused_computation.1 | custom fusion | bytes 12288 | tf_op jit(solution)/shard_map/jit(_take)/gather | solution.py:72
  475.5 4.0 gather_fusion.2
  479.5 1.4 copy.161
  481.7 2.6 select_select_fusion
  484.3 2.9 reduce-scatter.2.cloned.1.call-done
  487.2 1.7 fusion.39
  (81 shorter events, 7.5 us)
Async XLA Ops:
  7.2 8.4 %copy-start = (bf16[16,128,512]{2,1,0:T(8,128)(2,1)S(1)}, bf16[16,128,512]{2,1,0:T(8,128)(2,1)}, u32[]{:S(2)}) copy-start(bf16[16,128,512]{2,1,0:T(8,128)(2,1)} %param.27) | copy-start | bytes 6291460
  7.2 4.2 copy-start.4
  11.3 4.7 copy-start.9
  11.4 4.2 copy-start.11
  15.5 1.4 copy-start.5
  16.0 0.8 copy-start.6
  17.2 2.5 copy-start.15
  17.2 3.7 copy-start.3
  17.2 3.7 copy-start.7
  17.2 3.7 copy-start.10
  30.6 20.3 %copy-start.12 = (s32[4,1,32,6]{2,1,3,0:T(1,128)S(1)}, s32[4,1,32,6]{2,1,3,0:T(1,128)}, u32[]{:S(2)}) copy-start(s32[4,1,32,6]{2,1,3,0:T(1,128)} %param.31) | copy-start | bytes 9220
  30.6 20.6 %copy-start.14 = (bf16[2048]{0:T(1024)(128)(2,1)S(1)}, bf16[2048]{0:T(1024)(128)(2,1)}, u32[]{:S(2)}) copy-start(bf16[2048]{0:T(1024)(128)(2,1)} %param.30) | copy-start | bytes 12292
  46.5 10.9 %copy-start.8 = (bf16[1,32,2048]{2,1,0:T(8,128)(2,1)S(1)}, bf16[1,32,2048]{2,1,0:T(8,128)(2,1)}, u32[]{:S(2)}) copy-start(bf16[1,32,2048]{2,1,0:T(8,128)(2,1)} %param.18) | copy-start | bytes 393220
  46.5 10.4 %all-to-all-start = ((bf16[4,32,512]{2,1,0:T(8,128)(2,1)}), bf16[4,32,512]{2,1,0:T(8,128)(2,1)S(1)}, u32[]{:S(2)}, u32[]{:S(2)}) async-start(bf16[4,32,512]{2,1,0:T(8,128)(2,1)} %bitcast.14), calls=%async_computation | async-start | bytes 262144 | tf_op jit(solution)/shard_map/all_to_all | solution.py:123
  310.7 5.8 %copy-start.13 = (f32[4,1,32,6]{2,1,3,0:T(1,128)S(1)}, f32[4,1,32,6]{2,1,3,0:T(1,128)}, u32[]{:S(2)}) copy-start(f32[4,1,32,6]{2,1,3,0:T(1,128)} %param.32) | copy-start | bytes 9220
  310.7 5.8 %copy-start.16 = (s32[1,8]{1,0:T(1,128)S(1)}, s32[1,8]{1,0:T(1,128)}, u32[]{:S(2)}) copy-start(s32[1,8]{1,0:T(1,128)} %param.22) | copy-start | bytes 100
  310.7 147.0 %all-to-all-start.2 = ((bf16[64,4,6,2048]{3,1,2,0:T(4,128)(2,1)}), bf16[64,4,6,2048]{3,1,2,0:T(4,128)(2,1)}, u32[]{:S(2)}, u32[]{:S(2)}) async-start(bf16[64,4,6,2048]{3,1,2,0:T(4,128)(2,1)} %copy.159), calls=%async_computation.2 | async-start | bytes 12582912 | tf_op jit(solution)/shard_map/all_to_all | solution.py:146
  316.4 170.8 %reduce-scatter.2.cloned.1.call-start = ((), (), s32[]{:S(2)}) async-start(), calls=%async_computation.4 | async-start | bytes 655360 | tf_op jit(solution)/shard_map/reduce_scatter | solution.py:156
  468.2 0.7 copy-start.2
  481.7 7.2 %copy-start.1 = (bf16[16,128,512]{2,1,0:T(8,128)(2,1)S(1)}, bf16[16,128,512]{2,1,0:T(8,128)(2,1)}, u32[]{:S(2)}) copy-start(bf16[16,128,512]{2,1,0:T(8,128)(2,1)} %param.27) | copy-start | bytes 6291460
Sparse Core Ops, SparseCore 0:
  468.3 18.8 reduce-scatter.1
where the time goes:
time: 503 us; the launch traced here: 496 us
  blocking collectives  180 us (36%)
  waiting for transfers between devices  149 us (30%)
  local copies, waits for them, and re-layouts  82.8 us (16%)
  matrix products  45.8 us (9%)
  between operations  16 us (3%)
  other arithmetic  11.5 us (2%)
  starting transfers between devices  10.2 us (2%)
    all_to_all x1, blocking collectives, local(): lax.all_to_all(outbound, 'exp', split_axis=0, concat_axis=0, tiled=True)  153 us
    all_to_all x1, waiting for transfers between devices, local(): lax.all_to_all(jnp.dot(active, down_local, preferred_element_type=jnp.flo...  141 us
    reshape x2, local copies, waits for them, and re-layouts, local(): returned = lax.all_to_all(jnp.dot(active, down_local, preferred_element_t...  30.2 us
    all_gather x1, blocking collectives, local(): copies = lax.all_gather(normed[None], 'req', axis=0, tiled=True)  13.7 us
    all_gather x1, blocking collectives, local(): lax.all_gather(head_out, 'req', axis=0, tiled=True)  13.1 us
    dot_general x1, matrix products, local(): jnp.dot(active, down_local, preferred_element_type=jnp.float32)  12.2 us
    reshape x1, local copies, waits for them, and re-layouts, local(): flat = slot_block.reshape(-1, width)  11.1 us
    all_to_all x1, local copies, waits for them, and re-layouts, local(): lax.all_to_all(outbound, 'exp', split_axis=0, concat_axis=0, tiled=True)  10.7 us
  transfers between devices with their start and end apart: 3, of which 3 were waited for; matrix products, arithmetic and copies ran while one was open for 3% of the time, Pallas kernels for 0%

commit v1 on v0

--- a/solution.py
+++ b/solution.py
@@ -3,9 +3,23 @@
 import jax.numpy as jnp
 from jax import lax
 from jax.sharding import PartitionSpec as P
+from jax.lax import all_to_all, axis_size
 
 TOP = 6
 TREE = 32
+
+
+def _group_rates(dimension_no, work_x):
+    bus_axis = "req"
+    slots = axis_size(bus_axis)
+    column = [slots if c == dimension_no else 1 for c in range(work_x.ndim)]
+    return all_to_all(
+        jnp.tile(work_x, column),
+        bus_axis,
+        concat_axis=dimension_no,
+        split_axis=dimension_no,
+        tiled=True,
+    )
 
 
 def ancestry(parent_row):
@@ -116,9 +130,7 @@
         queries[0], pages, page_table[0], cache_len[0], parents[0], new_latent[0], key_up, value_up
     )
     column_block = jnp.dot(
-        lax.all_gather(head_out, "req", axis=0, tiled=True),
-        out_proj,
-        preferred_element_type=jnp.float32,
+        _group_rates(0, head_out), out_proj, preferred_element_type=jnp.float32
     ).astype(jnp.bfloat16)
     projected = lax.all_to_all(column_block, "req", split_axis=0, concat_axis=1, tiled=True)
     mixed = (hidden[0].astype(jnp.float32) + projected.astype(jnp.float32)).astype(jnp.bfloat16)

time: 503 us -> 503 us (level)
  blocking collectives: 180 us -> 166 us
  waiting for transfers between devices: 149 us -> 159 us
    all_gather x1 -> x0, blocking collectives: 13.1 us -> none  [local(): lax.all_gather(head_out, 'req', axis=0, tiled=True)]
    all_to_all x0 -> x1, waiting for transfers between devices: none -> 9.18 us  [_group_rates(): all_to_all(jnp.tile(work_x, column), bus_axis, concat_axis=dimension_no,...]
  transfers between devices with their start and end apart: 3 -> 4, of which waited for: 3 -> 4; matrix products, arithmetic and copies ran while one was open for 3% -> 3% of each run, Pallas kernels for 0% -> 0%
where the time goes in v1:
time: 503 us; the launch traced here: 496 us
  blocking collectives  166 us (33%)
  waiting for transfers between devices  159 us (32%)
  local copies, waits for them, and re-layouts  83.7 us (17%)
  matrix products  45.8 us (9%)
  between operations  16 us (3%)
  starting transfers between devices  13.6 us (3%)
  other arithmetic  11.5 us (2%)
    all_to_all x1, blocking collectives, local(): lax.all_to_all(outbound, 'exp', split_axis=0, concat_axis=0, tiled=True)  153 us
    all_to_all x1, waiting for transfers between devices, local(): lax.all_to_all(jnp.dot(active, down_local, preferred_element_type=jnp.flo...  141 us
    reshape x2, local copies, waits for them, and re-layouts, local(): returned = lax.all_to_all(jnp.dot(active, down_local, preferred_element_t...  30.2 us
    all_gather x1, blocking collectives, local(): copies = lax.all_gather(normed[None], 'req', axis=0, tiled=True)  13 us
    dot_general x1, matrix products, local(): jnp.dot(active, down_local, preferred_element_type=jnp.float32)  12.2 us
    reshape x1, local copies, waits for them, and re-layouts, local(): flat = slot_block.reshape(-1, width)  11 us
    all_to_all x1, local copies, waits for them, and re-layouts, local(): lax.all_to_all(outbound, 'exp', split_axis=0, concat_axis=0, tiled=True)  10.7 us
    dot_general x1, matrix products, local(): jnp.einsum('gxct,xgcd->gtd', weighted, returned.astype(jnp.float32))  10.5 us
  transfers between devices with their start and end apart: 4, of which 4 were waited for; matrix products, arithmetic and copies ran while one was open for 3% of the time, Pallas kernels for 0%

profile of v1, /device:TPU:8, one launch (start us, length us, event | category | flops | bytes accessed | tf_op | source)
XLA Modules:
  0.0 495.8 jit_solution(13725520204014004182)
XLA Ops:
  7.2 1.4 reshape_squeeze.3
  11.4 1.7 gather_fusion
  13.1 2.4 copy.166
  17.3 2.4 fusion.9
  21.8 2.1 fusion.10
  24.2 2.1 divide_convert_fusion
  26.3 1.8 fusion.24
  28.1 2.5 fusion.22
  31.5 4.4 all-to-all-start
  36.2 9.2 %all-to-all-done = bf16[4,32,2048]{2,1,0:T(8,128)(2,1)S(1)} async-done(((bf16[4,32,2048]{2,1,0:T(8,128)(2,1)}), bf16[4,32,2048]{2,1,0:T(8,128)(2,1)S(1)}, u32[]{:S(2)}, u32[]{:S(2)}) %all-to-all-start) | async-done | bytes 524320 | tf_op jit(solution)/shard_map/all_to_all | solution.py:16
  45.4 2.7 convolution_convert_fusion.2
  48.1 3.3 all-to-all-start.1
  51.5 5.9 %all-to-all-done.1 = bf16[4,32,512]{2,1,0:T(8,128)(2,1)S(1)} async-done(((bf16[4,32,512]{2,1,0:T(8,128)(2,1)}), bf16[4,32,512]{2,1,0:T(8,128)(2,1)S(1)}, u32[]{:S(2)}, u32[]{:S(2)}) %all-to-all-start.1) | async-done | bytes 131104 | tf_op jit(solution)/shard_map/all_to_all | solution.py:135
  58.1 13.0 %all_gather.3 = bf16[4,32,2048]{2,1,0:T(8,128)(2,1)S(1)} all-gather(bf16[1,32,2048]{2,1,0:T(8,128)(2,1)S(1)} %fusion.38), channel_id=1, replica_groups=mesh['req'=4,'exp'=64] {'req'}, dimensions={0}, use_global_device_ids=true | all-gather | bytes 655360 | tf_op jit(solution)/shard_map/all_gather | solution.py:148
  71.1 4.5 convert_bitcast_fusion
  75.6 10.3 %copy.157 = bf16[64,4,6,2048]{3,1,2,0:T(4,128)(2,1)} copy(bf16[64,4,6,2048]{3,0,2,1:T(8,128)(2,1)} %convert_bitcast_fusion) | data formatting | bytes 12582912 | tf_op jit(solution)/shard_map/convert_element_type | solution.py:152
  85.9 153.5 %all_to_all.32 = bf16[64,4,6,2048]{3,1,2,0:T(4,128)(2,1)S(1)} all-to-all(bf16[64,4,6,2048]{3,1,2,0:T(4,128)(2,1)} %copy.157), channel_id=1, replica_groups=mesh['req'=4,'exp'=64] {'exp'}, dimensions={0} | all-to-all | bytes 12582912 | tf_op jit(solution)/shard_map/all_to_all | solution.py:153
  239.3 10.7 %copy.158 = bf16[64,4,6,2048]{3,2,1,0:T(8,128)(2,1)} copy(bf16[64,4,6,2048]{3,1,2,0:T(4,128)(2,1)S(1)} %all_to_all.32) | data formatting | bytes 12582912 | tf_op jit(solution)/shard_map/all_to_all | solution.py:153
  250.1 11.0 %reshape.260 = bf16[1536,2048]{1,0:T(8,128)(2,1)} reshape(bf16[64,4,6,2048]{3,2,1,0:T(8,128)(2,1)} %copy.158) | data formatting | bytes 12582912 | tf_op jit(solution)/shard_map/reshape | solution.py:154
  261.1 7.0 %fusion.13 = f32[1536,352]{0,1:T(8,128)} fusion(bf16[1536,2048]{1,0:T(8,128)(2,1)} %reshape.260, bf16[1,2048,352]{1,2,0:T(8,128)(2,1)} %param.33), kind=kOutput, calls=%fused_computation.18 | convolution fusion | flops 2214592512 | bytes 9895936 | tf_op jit(solution)/shard_map/dot_general | solution.py:155
  268.1 12.2 %convolution_convert_fusion = bf16[1536,2048]{1,0:T(8,128)(2,1)} fusion(bf16[1,352,2048]{2,1,0:T(8,128)(2,1)} %param.35, bf16[1536,2048]{1,0:T(8,128)(2,1)} %reshape.260, f32[1536,352]{0,1:T(8,128)} %fusion.13, bf16[1,2048,352]{1,2,0:T(8,128)(2,1)} %param.34), kind=kOutput, calls=%fused_computation.3 | convolution fusion | flops 4435574784 | bytes 17629184 | tf_op jit(solution)/shard_map/dot_general | solution.py:159
  280.2 11.4 %reshape.261 = bf16[64,4,6,2048]{3,2,1,0:T(8,128)(2,1)} reshape(bf16[1536,2048]{1,0:T(8,128)(2,1)} %convolution_convert_fusion) | data formatting | bytes 12582912 | tf_op jit(solution)/shard_map/reshape | solution.py:161
  291.7 18.8 %copy.159 = bf16[64,4,6,2048]{3,1,2,0:T(4,128)(2,1)} copy(bf16[64,4,6,2048]{3,2,1,0:T(8,128)(2,1)} %reshape.261) | data formatting | bytes 12582912 | tf_op jit(solution)/shard_map/reshape | solution.py:161
  310.5 5.8 %all-to-all-start.3 = ((bf16[64,4,6,2048]{3,1,2,0:T(4,128)(2,1)}), bf16[64,4,6,2048]{3,1,2,0:T(4,128)(2,1)}, u32[]{:S(2)}, u32[]{:S(2)}) async-start(bf16[64,4,6,2048]{3,1,2,0:T(4,128)(2,1)} %copy.159), calls=%async_computation.3 | async-start | bytes 12582912 | tf_op jit(solution)/shard_map/all_to_all | solution.py:158
  316.7 140.8 %all-to-all-done.3 = bf16[64,4,6,2048]{3,1,2,0:T(4,128)(2,1)} async-done(((bf16[64,4,6,2048]{3,1,2,0:T(4,128)(2,1)}), bf16[64,4,6,2048]{3,1,2,0:T(4,128)(2,1)}, u32[]{:S(2)}, u32[]{:S(2)}) %all-to-all-start.3) | async-done | bytes 6291488 | tf_op jit(solution)/shard_map/all_to_all | solution.py:158
  457.5 10.5 %fusion.6 = bf16[4,32,2048]{2,1,0:T(8,128)(2,1)} fusion(bf16[64,4,6,2048]{3,1,2,0:T(4,128)(2,1)} %all-to-all-done.3, bf16[4,64,32]{1,2,0:T(8,128)(2,1)S(1)} %bitcast.130, s32[4,64,32]{1,2,0:T(8,128)S(1)} %subtract_bitcast_fusion, pred[4,64,32]{1,2,0:T(8,128)(4,1)S(1)} %compare_bitcast_fusion), kind=kOutput, calls=%fused_computation.10 | convolution fusion | flops 201474048 | bytes 6873088 | tf_op jit(solution)/shard_map/gxct,xgcd->gtd/dot_general | solution.py:167
  468.7 6.6 %gather_fusion.1 = s32[1024]{0:T(1024)S(1)} fusion(s32[32]{0:T(128)S(1)} %bitcast.121, s32[1024]{0:T(1024)S(1)} %bitcast_clamp_fusion), kind=kCustom, calls=%fused_computation.1 | custom fusion | bytes 12288 | tf_op jit(solution)/shard_map/jit(_take)/gather | solution.py:86
  475.3 4.0 gather_fusion.2
  479.4 1.4 copy.161
  481.6 2.6 select_select_fusion
  484.1 2.9 reduce-scatter.2.cloned.1.call-done
  487.1 1.7 fusion.39
  (83 shorter events, 9.1 us)
Async XLA Ops:
  7.2 8.4 %copy-start = (bf16[16,128,512]{2,1,0:T(8,128)(2,1)S(1)}, bf16[16,128,512]{2,1,0:T(8,128)(2,1)}, u32[]{:S(2)}) copy-start(bf16[16,128,512]{2,1,0:T(8,128)(2,1)} %param.27) | copy-start | bytes 6291460
  7.2 4.2 copy-start.4
  11.3 4.7 copy-start.9
  11.4 4.2 copy-start.11
  15.5 1.4 copy-start.5
  16.0 0.8 copy-start.6
  17.2 2.5 copy-start.15
  17.2 3.7 copy-start.3
  17.2 3.7 copy-start.7
  17.2 3.7 copy-start.10
  28.1 7.8 %copy-start.12 = (s32[4,1,32,6]{2,1,3,0:T(1,128)S(1)}, s32[4,1,32,6]{2,1,3,0:T(1,128)}, u32[]{:S(2)}) copy-start(s32[4,1,32,6]{2,1,3,0:T(1,128)} %param.31) | copy-start | bytes 9220
  31.5 20.0 %copy-start.14 = (bf16[2048]{0:T(1024)(128)(2,1)S(1)}, bf16[2048]{0:T(1024)(128)(2,1)}, u32[]{:S(2)}) copy-start(bf16[2048]{0:T(1024)(128)(2,1)} %param.30) | copy-start | bytes 12292
  31.5 13.9 %all-to-all-start = ((bf16[4,32,2048]{2,1,0:T(8,128)(2,1)}), bf16[4,32,2048]{2,1,0:T(8,128)(2,1)S(1)}, u32[]{:S(2)}, u32[]{:S(2)}) async-start(bf16[4,32,2048]{2,1,0:T(8,128)(2,1)} %tile.9), calls=%async_computation | async-start | bytes 1048576 | tf_op jit(solution)/shard_map/all_to_all | solution.py:16
  45.4 12.5 %copy-start.8 = (bf16[1,32,2048]{2,1,0:T(8,128)(2,1)S(1)}, bf16[1,32,2048]{2,1,0:T(8,128)(2,1)}, u32[]{:S(2)}) copy-start(bf16[1,32,2048]{2,1,0:T(8,128)(2,1)} %param.18) | copy-start | bytes 393220
  48.1 9.3 %all-to-all-start.1 = ((bf16[4,32,512]{2,1,0:T(8,128)(2,1)}), bf16[4,32,512]{2,1,0:T(8,128)(2,1)S(1)}, u32[]{:S(2)}, u32[]{:S(2)}) async-start(bf16[4,32,512]{2,1,0:T(8,128)(2,1)} %bitcast.15), calls=%async_computation.1 | async-start | bytes 262144 | tf_op jit(solution)/shard_map/all_to_all | solution.py:135
  310.5 5.8 %copy-start.13 = (f32[4,1,32,6]{2,1,3,0:T(1,128)S(1)}, f32[4,1,32,6]{2,1,3,0:T(1,128)}, u32[]{:S(2)}) copy-start(f32[4,1,32,6]{2,1,3,0:T(1,128)} %param.32) | copy-start | bytes 9220
  310.5 5.9 %copy-start.16 = (s32[1,8]{1,0:T(1,128)S(1)}, s32[1,8]{1,0:T(1,128)}, u32[]{:S(2)}) copy-start(s32[1,8]{1,0:T(1,128)} %param.22) | copy-start | bytes 100
  310.5 147.0 %all-to-all-start.3 = ((bf16[64,4,6,2048]{3,1,2,0:T(4,128)(2,1)}), bf16[64,4,6,2048]{3,1,2,0:T(4,128)(2,1)}, u32[]{:S(2)}, u32[]{:S(2)}) async-start(bf16[64,4,6,2048]{3,1,2,0:T(4,128)(2,1)} %copy.159), calls=%async_computation.3 | async-start | bytes 12582912 | tf_op jit(solution)/shard_map/all_to_all | solution.py:158
  316.2 170.8 %reduce-scatter.2.cloned.1.call-start = ((), (), s32[]{:S(2)}) async-start(), calls=%async_computation.5 | async-start | bytes 655360 | tf_op jit(solution)/shard_map/reduce_scatter | solution.py:168
  468.0 0.7 copy-start.2
  481.5 7.2 %copy-start.1 = (bf16[16,128,512]{2,1,0:T(8,128)(2,1)S(1)}, bf16[16,128,512]{2,1,0:T(8,128)(2,1)}, u32[]{:S(2)}) copy-start(bf16[16,128,512]{2,1,0:T(8,128)(2,1)} %param.27) | copy-start | bytes 6291460
Sparse Core Ops, SparseCore 0:
  468.2 18.8 reduce-scatter.1
